TPU v7x, 32 devices: a whole 2x2x4 slice. The times are simulated.
32 devices in a mesh: dp: 4 (over z), ctx: 8 (over y, x, core).
Axes of the slice: x: 2, y: 2, z: 4, core: 2. Of those that a mesh axis runs over, the one named last changes fastest.
Arguments:
- queries: bfloat16 [8192, 2048], P(('dp', 'ctx')), parts along dimension 0, may hold values from -256 to 256
- key_rows: bfloat16 [8192, 2048], P(('dp', 'ctx')), parts along dimension 0, may hold values from -256 to 256
- values: bfloat16 [8192, 2048], P(('dp', 'ctx')), parts along dimension 0, may hold values from -6 to 6
- inner_rows: bfloat16 [8192, 4096], P(('dp', 'ctx')), parts along dimension 0, may hold values from -6 to 6
- conv_weight: float32 [4, 4096], replicated, may hold values from -3 to 3
- conv_bias: float32 [4096], replicated, may hold values from -3 to 3
- segment_ids: int32 [8192], P(('dp', 'ctx')), parts along dimension 0, may hold values from 0 to 1, never falling along the last dimension, each value on 1 to 2047 neighbouring positions
- block_reach: int32 [64], P(('dp', 'ctx')), parts along dimension 0, may hold values from 128 to 2048
- owner_counts: int32 [32], P('dp'), parts along dimension 0, may hold values from 1 to 3, as said below
Outputs:
- attn_owned: bfloat16 [12288, 2048], P(('dp', 'ctx')), parts along dimension 0
- conv_owned: bfloat16 [12288, 4096], P(('dp', 'ctx')), parts along dimension 0
There are 4 independent parts, one for each index of `dp`. A program takes and returns all parts, laid end to end along the dimension named above; an argument that names none is the same for every part. Nothing has to cross between parts.
Inputs may be any that keep to these rules, and one draw needn't show every extreme that they name: `owner_counts`: the counts sum to 16. The blocks owned by the devices before device d number at least d * 2 and at most d * 2 + 1.
All inputs are finite; a program needn't handle non-finite values.
Results may differ from a plain program's by a relative error of at most 0.0047.
Values may be sent and summed in bfloat16 or wider, within the bound.
A program may use at most 192 MiB of HBM per device.

v0:
```python
import math

import jax
import jax.numpy as jnp
from jax import lax
from jax.sharding import PartitionSpec as P

HEADS = 16
D_HEAD = 128
WINDOW = 2048
BLOCK = 128
KERNEL = 4


masked_score = -1e30


def from_behind(block, axis, distance):
    devices = range(lax.axis_size(axis))
    route = [(i - distance, i) for i in devices if i - distance in devices]
    return lax.ppermute(block, axis, route)


def attend(query_rows, key_span, value_span, query_seg, key_seg, block_first, reach_value):
    query_pos = block_first + jnp.arange(BLOCK, dtype=jnp.int32)
    key_pos = block_first - WINDOW + jnp.arange(WINDOW + BLOCK, dtype=jnp.int32)
    allowed = (key_pos[None, :] <= query_pos[:, None]) & (
        key_pos[None, :] > query_pos[:, None] - WINDOW
    )
    allowed = allowed & (key_pos[None, :] >= block_first - reach_value) & (key_pos[None, :] >= 0)
    allowed = allowed & (key_seg[None, :] == query_seg[:, None])
    heads_q = query_rows.reshape(BLOCK, HEADS, D_HEAD)
    heads_k = key_span.reshape(WINDOW + BLOCK, HEADS, D_HEAD)
    heads_v = value_span.reshape(WINDOW + BLOCK, HEADS, D_HEAD)
    scores = jnp.einsum("qhd,khd->hqk", heads_q, heads_k, preferred_element_type=jnp.float32) * (
        1.0 / math.sqrt(D_HEAD)
    )
    scores = jnp.where(allowed[None], scores, masked_score)
    row_top = jnp.max(scores, axis=2, keepdims=True)
    lifted = jnp.where(allowed[None], jnp.exp(scores - row_top), 0.0)
    weights = (lifted / jnp.sum(lifted, axis=2, keepdims=True)).astype(jnp.bfloat16)
    mixed = jnp.einsum("hqk,khd->qhd", weights, heads_v, preferred_element_type=jnp.float32)
    return mixed.reshape(BLOCK, HEADS * D_HEAD).astype(jnp.bfloat16)


def convolve(ext_rows, ext_seg, ext_pos, conv_weight, conv_bias, row_count):
    lag = KERNEL - 1
    running = jnp.zeros((row_count, conv_bias.shape[0]), jnp.float32) + conv_bias[None, :]
    for offset in range(KERNEL):
        shifted = ext_rows[lag - offset : lag - offset + row_count].astype(jnp.float32)
        usable = (ext_seg[lag - offset : lag - offset + row_count] == ext_seg[lag:]) & (
            ext_pos[lag - offset : lag - offset + row_count] >= 0
        )
        running = running + conv_weight[offset][None, :] * jnp.where(usable[:, None], shifted, 0.0)
    return jax.nn.silu(running).astype(jnp.bfloat16)


def shards(
    queries,
    key_rows,
    values,
    inner_rows,
    conv_weight,
    conv_bias,
    segment_ids,
    block_reach,
    owner_counts,
):
    here_index = lax.axis_index("ctx")
    row_count = queries.shape[0]
    features = queries.shape[1]
    channels = inner_rows.shape[1]
    per_device = row_count // BLOCK
    most_blocks = per_device + per_device // 2
    back = WINDOW // row_count
    lag = KERNEL - 1
    starts = jnp.cumsum(owner_counts) - owner_counts
    first_block = starts[here_index]
    own_blocks = owner_counts[here_index]
    live = jnp.arange(most_blocks * BLOCK, dtype=jnp.int32) < own_blocks * BLOCK
    far_keys = []
    far_values = []
    far_segments = []
    for distance in range(back, 0, -1):
        received = from_behind((key_rows, values, segment_ids), "ctx", distance)
        far_keys.append(received[0])
        far_values.append(received[1])
        far_segments.append(received[2])
    key_buffer = jnp.concatenate(far_keys + [key_rows], axis=0)
    value_buffer = jnp.concatenate(far_values + [values], axis=0)
    segment_buffer = jnp.concatenate(far_segments + [segment_ids], axis=0)
    key_anchor = (here_index - back) * row_count
    tail_rows, tail_segments = from_behind(
        (inner_rows[row_count - lag :], segment_ids[row_count - lag :]), "ctx", 1
    )

    def own_block(slot_index):
        local_first = slot_index * BLOCK
        block_first = here_index * row_count + local_first
        key_at = block_first - WINDOW - key_anchor
        return attend(
            lax.dynamic_slice_in_dim(queries, local_first, BLOCK, 0),
            lax.dynamic_slice_in_dim(key_buffer, key_at, WINDOW + BLOCK, 0),
            lax.dynamic_slice_in_dim(value_buffer, key_at, WINDOW + BLOCK, 0),
            lax.dynamic_slice_in_dim(segment_ids, local_first, BLOCK, 0),
            lax.dynamic_slice_in_dim(segment_buffer, key_at, WINDOW + BLOCK, 0),
            block_first,
            block_reach[slot_index],
        )

    attention_local = lax.map(own_block, jnp.arange(per_device, dtype=jnp.int32)).reshape(
        row_count, features
    )
    conv_local = convolve(
        jnp.concatenate([tail_rows, inner_rows], axis=0),
        jnp.concatenate([tail_segments, segment_ids], axis=0),
        here_index * row_count - lag + jnp.arange(row_count + lag, dtype=jnp.int32),
        conv_weight,
        conv_bias,
        row_count,
    )
    above = from_behind((attention_local, conv_local), "ctx", -1)
    attention_near = jnp.concatenate(
        [attention_local, above[0], jnp.zeros((row_count, features), jnp.bfloat16)], axis=0
    )
    conv_near = jnp.concatenate(
        [conv_local, above[1], jnp.zeros((row_count, channels), jnp.bfloat16)], axis=0
    )
    offset_rows = first_block * BLOCK - here_index * row_count
    attention_owned = lax.dynamic_slice_in_dim(attention_near, offset_rows, most_blocks * BLOCK, 0)
    conv_owned_rows = lax.dynamic_slice_in_dim(conv_near, offset_rows, most_blocks * BLOCK, 0)
    attention_owned = jnp.where(live[:, None], attention_owned, 0)
    conv_owned_rows = jnp.where(live[:, None], conv_owned_rows, 0)
    return (attention_owned, conv_owned_rows)


def solution(mesh):
    return jax.shard_map(
        shards,
        mesh=mesh,
        in_specs=(
            P(("dp", "ctx"), None),
            P(("dp", "ctx"), None),
            P(("dp", "ctx"), None),
            P(("dp", "ctx"), None),
            P(),
            P(),
            P(("dp", "ctx")),
            P(("dp", "ctx")),
            P("dp"),
        ),
        out_specs=(P(("dp", "ctx"), None), P(("dp", "ctx"), None)),
        check_vma=False,
    )
```

profile of v0, /device:TPU:1, one launch (start us, length us, event | category | flops | bytes accessed | tf_op | source)
XLA Modules:
  0.0 383.7 jit_solution(14560332408308208776)
XLA Ops:
  5.4 5.5 %collective-permute-start.18 = (bf16[256,2048]{0,1:T(8,128)(2,1)S(1)}, bf16[256,2048]{0,1:T(8,128)(2,1)}, u32[]{:S(2)}, u32[]{:S(2)}) collective-permute-start(bf16[256,2048]{0,1:T(8,128)(2,1)S(1)} %copy.32), channel_id=1, source_target_pairs={{0,6},{1,7},{8,14},{9,15},{16,22},{17,23},{24,30},{25,31}} | collective-permute-start | bytes 3145736 | tf_op jit(solution)/shard_map/ppermute | solution.py:21
  10.9 2.3 collective-permute-start.19
  13.9 1.9 collective-permute-start.25
  19.3 35.4 %collective-permute-done.25 = s32[3]{0:T(128)S(1)} collective-permute-done((s32[3]{0:T(128)S(1)}, s32[3]{0:T(128)S(1)}, u32[]{:S(2)}, u32[]{:S(2)}) %collective-permute-start.25) | collective-permute-done | bytes 44 | tf_op jit(solution)/shard_map/ppermute | solution.py:21
  67.4 11.5 %collective-permute-start.14 = (s32[256]{0:T(256)}, s32[256]{0:T(256)S(1)}, u32[]{:S(2)}, u32[]{:S(2)}) collective-permute-start(s32[256]{0:T(256)} %param.17), channel_id=1, source_target_pairs={{0,2},{1,3},{2,4},{3,5},{4,6},{5,7},{8,10},{9,11},{10,12},{11,13},... | collective-permute-start | bytes 3080 | tf_op jit(solution)/shard_map/ppermute | solution.py:21
  79.9 4.2 %collective-permute-start.15 = (s32[256]{0:T(256)}, s32[256]{0:T(256)S(1)}, u32[]{:S(2)}, u32[]{:S(2)}) collective-permute-start(s32[256]{0:T(256)} %param.17), channel_id=1, source_target_pairs={{0,1},{1,2},{2,3},{3,4},{4,5},{5,6},{6,7},{8,9},{9,10},{10,11},{11... | collective-permute-start | bytes 3080 | tf_op jit(solution)/shard_map/ppermute | solution.py:21
  85.0 4.2 %collective-permute-start.26 = (bf16[3,4096]{1,0:T(4,128)(2,1)S(1)}, bf16[3,4096]{1,0:T(4,128)(2,1)S(1)}, u32[]{:S(2)}, u32[]{:S(2)}) collective-permute-start(bf16[3,4096]{1,0:T(4,128)(2,1)S(1)} %slice.54), channel_id=1, source_target_pairs={{0,1},{1,2},{2,3},{3,4},{4,5},{5,6},{6,7},{8,9},{9,10},{10,11},{11... | collective-permute-start | bytes 73736 | tf_op jit(solution)/shard_map/ppermute | solution.py:21
  90.2 4.4 %collective-permute-start.20 = (bf16[256,2048]{0,1:T(8,128)(2,1)S(1)}, bf16[256,2048]{0,1:T(8,128)(2,1)S(1)}, u32[]{:S(2)}, u32[]{:S(2)}) collective-permute-start(bf16[256,2048]{0,1:T(8,128)(2,1)S(1)} %copy.32), channel_id=1, source_target_pairs={{0,4},{1,5},{2,6},{3,7},{8,12},{9,13},{10,14},{11,15},{16,20},{17,... | collective-permute-start | bytes 3145736 | tf_op jit(solution)/shard_map/ppermute | solution.py:21
  94.6 9.8 %multiply_convert_fusion = bf16[256,4096]{1,0:T(8,128)(2,1)} fusion(bf16[256,4096]{1,0:T(8,128)(2,1)} %param.14, bf16[3,4096]{1,0:T(4,128)(2,1)S(1)} %collective-permute-done.26, f32[4096]{0:T(1024)S(1)} %bitcast.49, f32[4096]{0:T(1024)S(1)} %bitcast.50, f32[4096]{0:T(1024)S(1)} %bitcast.48, f32[4096]{0:T(1024)S(1)} %bitcast.47, f32[4096]{0:T(1024)} %param.16, ...), kind=kLoop, calls=%fused_computation.25 | loop fusion | flops 31457280 | bytes 4301824 | tf_op jit(solution)/shard_map/convert_element_type | solution.py:55
  104.4 4.7 %collective-permute-start.21 = (bf16[256,2048]{0,1:T(8,128)(2,1)S(1)}, bf16[256,2048]{0,1:T(8,128)(2,1)S(1)}, u32[]{:S(2)}, u32[]{:S(2)}) collective-permute-start(bf16[256,2048]{0,1:T(8,128)(2,1)S(1)} %copy.32), channel_id=1, source_target_pairs={{0,3},{1,4},{2,5},{3,6},{4,7},{8,11},{9,12},{10,13},{11,14},{12,15... | collective-permute-start | bytes 3145736 | tf_op jit(solution)/shard_map/ppermute | solution.py:21
  113.1 3.9 %collective-permute-start.23 = (bf16[256,2048]{0,1:T(8,128)(2,1)S(1)}, bf16[256,2048]{0,1:T(8,128)(2,1)S(1)}, u32[]{:S(2)}, u32[]{:S(2)}) collective-permute-start(bf16[256,2048]{0,1:T(8,128)(2,1)S(1)} %copy.32), channel_id=1, source_target_pairs={{0,1},{1,2},{2,3},{3,4},{4,5},{5,6},{6,7},{8,9},{9,10},{10,11},{11... | collective-permute-start | bytes 3145736 | tf_op jit(solution)/shard_map/ppermute | solution.py:21
  120.3 38.1 %collective-permute-done.20 = bf16[256,2048]{0,1:T(8,128)(2,1)S(1)} collective-permute-done((bf16[256,2048]{0,1:T(8,128)(2,1)S(1)}, bf16[256,2048]{0,1:T(8,128)(2,1)S(1)}, u32[]{:S(2)}, u32[]{:S(2)}) %collective-permute-start.20) | collective-permute-done | bytes 1048608 | tf_op jit(solution)/shard_map/ppermute | solution.py:21
  159.2 41.4 %collective-permute-done.21 = bf16[256,2048]{0,1:T(8,128)(2,1)S(1)} collective-permute-done((bf16[256,2048]{0,1:T(8,128)(2,1)S(1)}, bf16[256,2048]{0,1:T(8,128)(2,1)S(1)}, u32[]{:S(2)}, u32[]{:S(2)}) %collective-permute-start.21) | collective-permute-done | bytes 1048608 | tf_op jit(solution)/shard_map/ppermute | solution.py:21
  205.1 3.1 collective-permute-start.5
  209.7 8.4 %collective-permute-done.2 = bf16[256,2048]{0,1:T(8,128)(2,1)S(1)} collective-permute-done((bf16[256,2048]{0,1:T(8,128)(2,1)S(1)}, bf16[256,2048]{0,1:T(8,128)(2,1)S(1)}, u32[]{:S(2)}, u32[]{:S(2)}) %collective-permute-start.2) | collective-permute-done | bytes 1048608 | tf_op jit(solution)/shard_map/ppermute | solution.py:21
  218.1 1.9 collective-permute-start.7
  220.2 20.4 %collective-permute-done.3 = bf16[256,2048]{0,1:T(8,128)(2,1)S(1)} collective-permute-done((bf16[256,2048]{0,1:T(8,128)(2,1)S(1)}, bf16[256,2048]{0,1:T(8,128)(2,1)S(1)}, u32[]{:S(2)}, u32[]{:S(2)}) %collective-permute-start.3) | collective-permute-done | bytes 1048608 | tf_op jit(solution)/shard_map/ppermute | solution.py:21
  240.6 2.1 collective-permute-start.27
  242.8 7.5 %collective-permute-done.4 = bf16[256,2048]{0,1:T(8,128)(2,1)S(1)} collective-permute-done((bf16[256,2048]{0,1:T(8,128)(2,1)S(1)}, bf16[256,2048]{0,1:T(8,128)(2,1)S(1)}, u32[]{:S(2)}, u32[]{:S(2)}) %collective-permute-start.4) | collective-permute-done | bytes 1048608 | tf_op jit(solution)/shard_map/ppermute | solution.py:21
  250.3 13.2 %collective-permute-done.5 = bf16[256,2048]{0,1:T(8,128)(2,1)S(1)} collective-permute-done((bf16[256,2048]{0,1:T(8,128)(2,1)S(1)}, bf16[256,2048]{0,1:T(8,128)(2,1)S(1)}, u32[]{:S(2)}, u32[]{:S(2)}) %collective-permute-start.5) | collective-permute-done | bytes 1048608 | tf_op jit(solution)/shard_map/ppermute | solution.py:21
  263.7 6.2 %collective-permute-done.7 = bf16[256,2048]{0,1:T(8,128)(2,1)S(1)} collective-permute-done((bf16[256,2048]{0,1:T(8,128)(2,1)S(1)}, bf16[256,2048]{0,1:T(8,128)(2,1)S(1)}, u32[]{:S(2)}, u32[]{:S(2)}) %collective-permute-start.7) | collective-permute-done | bytes 1048608 | tf_op jit(solution)/shard_map/ppermute | solution.py:21
  270.1 3.6 copy-done.1
  273.6 84.7 %while.13 = (s32[]{:T(128)}, bf16[2,128,2048]{2,1,0:T(8,128)(2,1)S(1)}, s32[2]{0:T(128)S(1)}, s32[]{:T(128)}, s32[]{:T(128)}, /*index=5*/bf16[2304,2048]{0,1:T(8...) while((s32[]{:T(128)}, ...), condition=%wide.region_3.4_spmd, body=%wide.region_0.3_spmd.sunk | while | flops 2315119616 | bytes 95001464 | solution.py:111
  278.4 12.0 %constant_dynamic-slice_fusion.5 = (bf16[2176,2048]{0,1:T(8,128)(2,1)}, bf16[2176,2048]{0,1:T(8,128)(2,1)}) fusion(bf16[2304,2048]{0,1:T(8,128)(2,1)} %get-tuple-element.350, s32[]{:T(128)S(6)} %select_n.98, bf16[2304,2048]{0,1:T(8,128)(2,1)} %get-tuple-element.345), kind=kLoop, calls=%fused_computation.16.clone.1 | loop fusion | bytes 35651588 | tf_op jit(solution)/shard_map/while/body/eval_jaxpr/dynamic_slice | solution.py:103
  290.7 13.6 %fusion.38 = (f32[16,128]{1,0:T(8,128)S(1)}, f32[16,128,2176]{2,1,0:T(8,128)}) fusion(pred[128,2176]{1,0:T(8,128)(4,1)S(1)} %compare_and_fusion.5, bf16[128,16,128]{0,2,1:T(8,128)(2,1)S(1)} %bitcast.43, bf16[2176,16,128]{0,2,1:T(8,128)(2,1)} %bitcast.42), kind=kOutput, calls=%fused_computation.75.clone.1 | convolution fusion | flops 1163135104 | bytes 27549696 | tf_op jit(solution)/shard_map/while/body/eval_jaxpr/sub | solution.py:40
  304.3 11.4 %fusion.39 = bf16[16,128,128]{2,1,0:T(8,128)(2,1)S(1)} fusion(bf16[2176,16,128]{0,2,1:T(8,128)(2,1)} %bitcast.41, f32[16,128,2176]{2,1,0:T(8,128)} %get-tuple-element.302, f32[16,128]{1,0:T(8,128)S(1)} %get-tuple-element.303), kind=kOutput, calls=%fused_computation.10.clone.1 | convolution fusion | flops 1150025728 | bytes 27271168 | tf_op jit(solution)/shard_map/while/body/eval_jaxpr/hqk,khd->qhd/dot_general | solution.py:42
  320.8 12.0 %constant_dynamic-slice_fusion.5 = (bf16[2176,2048]{0,1:T(8,128)(2,1)}, bf16[2176,2048]{0,1:T(8,128)(2,1)}) fusion(bf16[2304,2048]{0,1:T(8,128)(2,1)} %get-tuple-element.350, s32[]{:T(128)S(6)} %select_n.98, bf16[2304,2048]{0,1:T(8,128)(2,1)} %get-tuple-element.345), kind=kLoop, calls=%fused_computation.16.clone.1 | loop fusion | bytes 35651588 | tf_op jit(solution)/shard_map/while/body/eval_jaxpr/dynamic_slice | solution.py:103
  333.1 13.6 %fusion.38 = (f32[16,128]{1,0:T(8,128)S(1)}, f32[16,128,2176]{2,1,0:T(8,128)}) fusion(pred[128,2176]{1,0:T(8,128)(4,1)S(1)} %compare_and_fusion.5, bf16[128,16,128]{0,2,1:T(8,128)(2,1)S(1)} %bitcast.43, bf16[2176,16,128]{0,2,1:T(8,128)(2,1)} %bitcast.42), kind=kOutput, calls=%fused_computation.75.clone.1 | convolution fusion | flops 1163135104 | bytes 27549696 | tf_op jit(solution)/shard_map/while/body/eval_jaxpr/sub | solution.py:40
  346.7 11.4 %fusion.39 = bf16[16,128,128]{2,1,0:T(8,128)(2,1)S(1)} fusion(bf16[2176,16,128]{0,2,1:T(8,128)(2,1)} %bitcast.41, f32[16,128,2176]{2,1,0:T(8,128)} %get-tuple-element.302, f32[16,128]{1,0:T(8,128)S(1)} %get-tuple-element.303), kind=kOutput, calls=%fused_computation.10.clone.1 | convolution fusion | flops 1150025728 | bytes 27271168 | tf_op jit(solution)/shard_map/while/body/eval_jaxpr/hqk,khd->qhd/dot_general | solution.py:42
  358.4 2.1 collective-permute-start.24
  363.2 12.0 %collective-permute-done.24 = bf16[256,2048]{1,0:T(8,128)(2,1)S(1)} collective-permute-done((bf16[256,2048]{1,0:T(8,128)(2,1)S(1)}, bf16[256,2048]{1,0:T(8,128)(2,1)S(1)}, u32[]{:S(2)}, u32[]{:S(2)}) %collective-permute-start.24) | collective-permute-done | bytes 1048608 | tf_op jit(solution)/shard_map/ppermute | solution.py:21
  377.1 6.6 %fusion.15 = bf16[384,4096]{1,0:T(8,128)(2,1)} fusion(s32[]{:T(128)S(6)} %select_n.69, bf16[256,4096]{1,0:T(8,128)(2,1)} %multiply_convert_fusion, bf16[256,4096]{1,0:T(8,128)(2,1)} %collective-permute-done.27, pred[384]{0:T(512)(128)(4,1)S(1)} %iota_compare_fusion, bf16[384]{0:T(512)(128)(2,1)S(1)} %pad_dynamic-slice_fusion.4), kind=kLoop, calls=%fused_computation.28 | loop fusion | flops 11010048 | bytes 7341188 | tf_op jit(solution)/shard_map/jit(_where)/select_n | solution.py:133
  (115 shorter events, 46.9 us)
Async XLA Ops:
  2.1 102.3 %collective-permute-start.16 = (bf16[256,2048]{0,1:T(8,128)(2,1)S(1)}, bf16[256,2048]{0,1:T(8,128)(2,1)}, u32[]{:S(2)}, u32[]{:S(2)}) collective-permute-start(bf16[256,2048]{0,1:T(8,128)(2,1)S(1)} %copy.32), channel_id=1, source_target_pairs={} | collective-permute-start | bytes 3145736 | tf_op jit(solution)/shard_map/ppermute | solution.py:21
  3.8 106.6 %collective-permute-start.17 = (bf16[256,2048]{0,1:T(8,128)(2,1)S(1)}, bf16[256,2048]{0,1:T(8,128)(2,1)}, u32[]{:S(2)}, u32[]{:S(2)}) collective-permute-start(bf16[256,2048]{0,1:T(8,128)(2,1)S(1)} %copy.32), channel_id=1, source_target_pairs={{0,7},{8,15},{16,23},{24,31}} | collective-permute-start | bytes 3145736 | tf_op jit(solution)/shard_map/ppermute | solution.py:21
  5.4 107.7 %collective-permute-start.18 = (bf16[256,2048]{0,1:T(8,128)(2,1)S(1)}, bf16[256,2048]{0,1:T(8,128)(2,1)}, u32[]{:S(2)}, u32[]{:S(2)}) collective-permute-start(bf16[256,2048]{0,1:T(8,128)(2,1)S(1)} %copy.32), channel_id=1, source_target_pairs={{0,6},{1,7},{8,14},{9,15},{16,22},{17,23},{24,30},{25,31}} | collective-permute-start | bytes 3145736 | tf_op jit(solution)/shard_map/ppermute | solution.py:21
  10.9 107.3 %collective-permute-start.19 = (bf16[256,2048]{0,1:T(8,128)(2,1)S(1)}, bf16[256,2048]{0,1:T(8,128)(2,1)}, u32[]{:S(2)}, u32[]{:S(2)}) collective-permute-start(bf16[256,2048]{0,1:T(8,128)(2,1)S(1)} %copy.32), channel_id=1, source_target_pairs={{0,5},{1,6},{2,7},{8,13},{9,14},{10,15},{16,21},{17,22},{18,23},{2... | collective-permute-start | bytes 3145736 | tf_op jit(solution)/shard_map/ppermute | solution.py:21
  13.9 40.8 %collective-permute-start.25 = (s32[3]{0:T(128)S(1)}, s32[3]{0:T(128)S(1)}, u32[]{:S(2)}, u32[]{:S(2)}) collective-permute-start(s32[3]{0:T(128)S(1)} %slice.51), channel_id=1, source_target_pairs={{0,1},{1,2},{2,3},{3,4},{4,5},{5,6},{6,7},{8,9},{9,10},{10,11},{11... | collective-permute-start | bytes 44 | tf_op jit(solution)/shard_map/ppermute | solution.py:21
  54.7 2.2 collective-permute-start.8
  56.9 0.7 collective-permute-start.9
  57.6 2.4 collective-permute-start.10
  60.0 2.8 collective-permute-start.11
  62.8 2.2 collective-permute-start.12
  65.0 2.4 collective-permute-start.13
  67.4 12.4 %collective-permute-start.14 = (s32[256]{0:T(256)}, s32[256]{0:T(256)S(1)}, u32[]{:S(2)}, u32[]{:S(2)}) collective-permute-start(s32[256]{0:T(256)} %param.17), channel_id=1, source_target_pairs={{0,2},{1,3},{2,4},{3,5},{4,6},{5,7},{8,10},{9,11},{10,12},{11,13},... | collective-permute-start | bytes 3080 | tf_op jit(solution)/shard_map/ppermute | solution.py:21
  79.9 5.1 %collective-permute-start.15 = (s32[256]{0:T(256)}, s32[256]{0:T(256)S(1)}, u32[]{:S(2)}, u32[]{:S(2)}) collective-permute-start(s32[256]{0:T(256)} %param.17), channel_id=1, source_target_pairs={{0,1},{1,2},{2,3},{3,4},{4,5},{5,6},{6,7},{8,9},{9,10},{10,11},{11... | collective-permute-start | bytes 3080 | tf_op jit(solution)/shard_map/ppermute | solution.py:21
  85.0 5.2 %collective-permute-start.26 = (bf16[3,4096]{1,0:T(4,128)(2,1)S(1)}, bf16[3,4096]{1,0:T(4,128)(2,1)S(1)}, u32[]{:S(2)}, u32[]{:S(2)}) collective-permute-start(bf16[3,4096]{1,0:T(4,128)(2,1)S(1)} %slice.54), channel_id=1, source_target_pairs={{0,1},{1,2},{2,3},{3,4},{4,5},{5,6},{6,7},{8,9},{9,10},{10,11},{11... | collective-permute-start | bytes 73736 | tf_op jit(solution)/shard_map/ppermute | solution.py:21
  90.2 68.2 %collective-permute-start.20 = (bf16[256,2048]{0,1:T(8,128)(2,1)S(1)}, bf16[256,2048]{0,1:T(8,128)(2,1)S(1)}, u32[]{:S(2)}, u32[]{:S(2)}) collective-permute-start(bf16[256,2048]{0,1:T(8,128)(2,1)S(1)} %copy.32), channel_id=1, source_target_pairs={{0,4},{1,5},{2,6},{3,7},{8,12},{9,13},{10,14},{11,15},{16,20},{17,... | collective-permute-start | bytes 3145736 | tf_op jit(solution)/shard_map/ppermute | solution.py:21
  104.4 96.3 %collective-permute-start.21 = (bf16[256,2048]{0,1:T(8,128)(2,1)S(1)}, bf16[256,2048]{0,1:T(8,128)(2,1)S(1)}, u32[]{:S(2)}, u32[]{:S(2)}) collective-permute-start(bf16[256,2048]{0,1:T(8,128)(2,1)S(1)} %copy.32), channel_id=1, source_target_pairs={{0,3},{1,4},{2,5},{3,6},{4,7},{8,11},{9,12},{10,13},{11,14},{12,15... | collective-permute-start | bytes 3145736 | tf_op jit(solution)/shard_map/ppermute | solution.py:21
  110.4 91.7 %collective-permute-start.22 = (bf16[256,2048]{0,1:T(8,128)(2,1)S(1)}, bf16[256,2048]{0,1:T(8,128)(2,1)S(1)}, u32[]{:S(2)}, u32[]{:S(2)}) collective-permute-start(bf16[256,2048]{0,1:T(8,128)(2,1)S(1)} %copy.32), channel_id=1, source_target_pairs={{0,2},{1,3},{2,4},{3,5},{4,6},{5,7},{8,10},{9,11},{10,12},{11,13},... | collective-permute-start | bytes 3145736 | tf_op jit(solution)/shard_map/ppermute | solution.py:21
  113.1 90.5 %collective-permute-start.23 = (bf16[256,2048]{0,1:T(8,128)(2,1)S(1)}, bf16[256,2048]{0,1:T(8,128)(2,1)S(1)}, u32[]{:S(2)}, u32[]{:S(2)}) collective-permute-start(bf16[256,2048]{0,1:T(8,128)(2,1)S(1)} %copy.32), channel_id=1, source_target_pairs={{0,1},{1,2},{2,3},{3,4},{4,5},{5,6},{6,7},{8,9},{9,10},{10,11},{11... | collective-permute-start | bytes 3145736 | tf_op jit(solution)/shard_map/ppermute | solution.py:21
  118.3 86.8 %collective-permute-start = (bf16[256,2048]{0,1:T(8,128)(2,1)S(1)}, bf16[256,2048]{0,1:T(8,128)(2,1)S(1)}, u32[]{:S(2)}, u32[]{:S(2)}) collective-permute-start(bf16[256,2048]{0,1:T(8,128)(2,1)S(1)} %copy.23), channel_id=1, source_target_pairs={} | collective-permute-start | bytes 3145736 | tf_op jit(solution)/shard_map/ppermute | solution.py:21
  158.4 49.9 %collective-permute-start.1 = (bf16[256,2048]{0,1:T(8,128)(2,1)S(1)}, bf16[256,2048]{0,1:T(8,128)(2,1)S(1)}, u32[]{:S(2)}, u32[]{:S(2)}) collective-permute-start(bf16[256,2048]{0,1:T(8,128)(2,1)S(1)} %copy.23), channel_id=1, source_target_pairs={{0,7},{8,15},{16,23},{24,31}} | collective-permute-start | bytes 3145736 | tf_op jit(solution)/shard_map/ppermute | solution.py:21
  200.6 17.5 %collective-permute-start.2 = (bf16[256,2048]{0,1:T(8,128)(2,1)S(1)}, bf16[256,2048]{0,1:T(8,128)(2,1)S(1)}, u32[]{:S(2)}, u32[]{:S(2)}) collective-permute-start(bf16[256,2048]{0,1:T(8,128)(2,1)S(1)} %copy.23), channel_id=1, source_target_pairs={{0,6},{1,7},{8,14},{9,15},{16,22},{17,23},{24,30},{25,31}} | collective-permute-start | bytes 3145736 | tf_op jit(solution)/shard_map/ppermute | solution.py:21
  202.1 38.5 %collective-permute-start.3 = (bf16[256,2048]{0,1:T(8,128)(2,1)S(1)}, bf16[256,2048]{0,1:T(8,128)(2,1)S(1)}, u32[]{:S(2)}, u32[]{:S(2)}) collective-permute-start(bf16[256,2048]{0,1:T(8,128)(2,1)S(1)} %copy.23), channel_id=1, source_target_pairs={{0,5},{1,6},{2,7},{8,13},{9,14},{10,15},{16,21},{17,22},{18,23},{2... | collective-permute-start | bytes 3145736 | tf_op jit(solution)/shard_map/ppermute | solution.py:21
  203.5 46.7 %collective-permute-start.4 = (bf16[256,2048]{0,1:T(8,128)(2,1)S(1)}, bf16[256,2048]{0,1:T(8,128)(2,1)S(1)}, u32[]{:S(2)}, u32[]{:S(2)}) collective-permute-start(bf16[256,2048]{0,1:T(8,128)(2,1)S(1)} %copy.23), channel_id=1, source_target_pairs={{0,4},{1,5},{2,6},{3,7},{8,12},{9,13},{10,14},{11,15},{16,20},{17,... | collective-permute-start | bytes 3145736 | tf_op jit(solution)/shard_map/ppermute | solution.py:21
  205.1 58.5 %copy-start = (bf16[2304,2048]{0,1:T(8,128)(2,1)}, bf16[2304,2048]{0,1:T(8,128)(2,1)S(1)}, u32[]{:S(2)}) copy-start(bf16[2304,2048]{0,1:T(8,128)(2,1)S(1)} %constant_dynamic-update-slice_fusion.11) | copy-start | bytes 28311556
  205.1 58.4 %collective-permute-start.5 = (bf16[256,2048]{0,1:T(8,128)(2,1)S(1)}, bf16[256,2048]{0,1:T(8,128)(2,1)S(1)}, u32[]{:S(2)}, u32[]{:S(2)}) collective-permute-start(bf16[256,2048]{0,1:T(8,128)(2,1)S(1)} %copy.23), channel_id=1, source_target_pairs={{0,3},{1,4},{2,5},{3,6},{4,7},{8,11},{9,12},{10,13},{11,14},{12,15... | collective-permute-start | bytes 3145736 | tf_op jit(solution)/shard_map/ppermute | solution.py:21
  208.3 55.3 %collective-permute-start.6 = (bf16[256,2048]{0,1:T(8,128)(2,1)S(1)}, bf16[256,2048]{0,1:T(8,128)(2,1)S(1)}, u32[]{:S(2)}, u32[]{:S(2)}) collective-permute-start(bf16[256,2048]{0,1:T(8,128)(2,1)S(1)} %copy.23), channel_id=1, source_target_pairs={{0,2},{1,3},{2,4},{3,5},{4,6},{5,7},{8,10},{9,11},{10,12},{11,13},... | collective-permute-start | bytes 3145736 | tf_op jit(solution)/shard_map/ppermute | solution.py:21
  218.1 51.8 %collective-permute-start.7 = (bf16[256,2048]{0,1:T(8,128)(2,1)S(1)}, bf16[256,2048]{0,1:T(8,128)(2,1)S(1)}, u32[]{:S(2)}, u32[]{:S(2)}) collective-permute-start(bf16[256,2048]{0,1:T(8,128)(2,1)S(1)} %copy.23), channel_id=1, source_target_pairs={{0,1},{1,2},{2,3},{3,4},{4,5},{5,6},{6,7},{8,9},{9,10},{10,11},{11... | collective-permute-start | bytes 3145736 | tf_op jit(solution)/shard_map/ppermute | solution.py:21
  220.1 53.5 %copy-start.2 = (bf16[256,2048]{1,0:T(8,128)(2,1)S(1)}, bf16[256,2048]{1,0:T(8,128)(2,1)}, u32[]{:S(2)}) copy-start(bf16[256,2048]{1,0:T(8,128)(2,1)} %param.11) | copy-start | bytes 3145732
  220.1 53.5 %copy-start.3 = (s32[256]{0:T(256)S(1)}, s32[256]{0:T(256)}, u32[]{:S(2)}) copy-start(s32[256]{0:T(256)} %param.17) | copy-start | bytes 3076
  240.6 136.5 %collective-permute-start.27 = (bf16[256,4096]{1,0:T(8,128)(2,1)}, bf16[256,4096]{1,0:T(8,128)(2,1)}, u32[]{:S(2)}, u32[]{:S(2)}) collective-permute-start(bf16[256,4096]{1,0:T(8,128)(2,1)} %multiply_convert_fusion), channel_id=1, source_target_pairs={{1,0},{2,1},{3,2},{4,3},{5,4},{6,5},{7,6},{9,8},{10,9},{11,10},{12... | collective-permute-start | bytes 6291464 | tf_op jit(solution)/shard_map/ppermute | solution.py:21
  273.6 86.9 %copy-start.5 = (s32[8]{0:T(128)S(1)}, s32[8]{0:T(128)}, u32[]{:S(2)}) copy-start(s32[8]{0:T(128)} %param.19) | copy-start | bytes 100
  358.4 16.8 %collective-permute-start.24 = (bf16[256,2048]{1,0:T(8,128)(2,1)S(1)}, bf16[256,2048]{1,0:T(8,128)(2,1)S(1)}, u32[]{:S(2)}, u32[]{:S(2)}) collective-permute-start(bf16[256,2048]{1,0:T(8,128)(2,1)S(1)} %bitcast.45), channel_id=1, source_target_pairs={{1,0},{2,1},{3,2},{4,3},{5,4},{6,5},{7,6},{9,8},{10,9},{11,10},{12... | collective-permute-start | bytes 3145736 | tf_op jit(solution)/shard_map/ppermute | solution.py:21
  (2 other events, 57.0 us)
where the time goes:
time: 385 us; the launch traced here: 384 us
  waiting for transfers between devices  188 us (49%)
  starting transfers between devices  70.7 us (18%)
  matrix products  50 us (13%)
  local copies, waits for them, and re-layouts  45 us (12%)
  other arithmetic  21.1 us (5%)
  loops' own time  5.89 us (2%)
    ppermute x28, waiting for transfers between devices, from_behind(): return lax.ppermute(block, axis, route)  188 us
    ppermute x28, starting transfers between devices, from_behind(): return lax.ppermute(block, axis, route)  70.7 us
    sub x2, matrix products, attend(): lifted = jnp.where(allowed[None], jnp.exp(scores - row_top), 0.0)  27.2 us
    dynamic_slice x2, local copies, waits for them, and re-layouts, own_block(): lax.dynamic_slice_in_dim(key_buffer, key_at, WINDOW + BLOCK, 0)  23.9 us
    dot_general x2, matrix products, attend(): jnp.einsum('hqk,khd->qhd', weights, heads_v, preferred_element_type=jnp.f...  22.8 us
    unnamed x38, local copies, waits for them, and re-layouts  12.6 us
    convert_element_type x1, other arithmetic, convolve(): return jax.nn.silu(running).astype(jnp.bfloat16)  9.83 us
  transfers between devices with their start and end apart: 28, of which 16 were waited for; matrix products, arithmetic and copies ran while one was open for 27% of the time, Pallas kernels for 0%

commit v1 on v0

--- a/solution.py
+++ b/solution.py
@@ -1,8 +1,11 @@
+import functools
 import math
 
 import jax
 import jax.numpy as jnp
 from jax import lax
+from jax.experimental import pallas as pl
+from jax.experimental.pallas import tpu as pltpu
 from jax.sharding import PartitionSpec as P
 
 HEADS = 16
@@ -134,9 +137,405 @@
     return (attention_owned, conv_owned_rows)
 
 
+LANES = 128
+HALO = 16
+MESH = pl.DeviceIdType.MESH
+
+
+def partner(me, offset, n):
+    result, bit = 0, 1
+    while bit < n:
+        result = result + ((me // bit + offset // bit) % 2) * bit
+        bit *= 2
+    return result
+
+
+def exchange_kernel(
+    n,
+    row_count,
+    head_count,
+    q_hbm,
+    k_hbm,
+    v_hbm,
+    x_hbm,
+    weight_ref,
+    bias_ref,
+    info_ref,
+    attn_near,
+    conv_near,
+    qr,
+    kr,
+    vr,
+    ob,
+    xb,
+    infos,
+    start_ref,
+    lo_ref,
+    s_ref,
+    qkv_send,
+    qkv_recv,
+    o_send,
+    o_recv,
+    info_send,
+    info_recv,
+    halo_sem,
+    local_sem,
+):
+    me = lax.axis_index("ctx")
+    per_device = row_count // BLOCK
+    near = row_count + BLOCK
+    seq_len = n * row_count
+    channels = bias_ref.shape[1]
+    chunk = s_ref.shape[2]
+    scale = math.log2(math.e) / math.sqrt(D_HEAD)
+    order = list(range(2, n)) + [1]
+
+    barrier = pltpu.get_barrier_semaphore()
+    for offset in range(1, n):
+        pl.semaphore_signal(
+            barrier, inc=1, device_id={"ctx": partner(me, offset, n)}, device_id_type=MESH
+        )
+    pl.semaphore_wait(barrier, n - 1)
+
+    def rows_of(device, count=row_count):
+        return pl.ds(pl.multiple_of(device * row_count, BLOCK), count)
+
+    def head_of(device, head):
+        at = device * (head_count * D_HEAD) + head * D_HEAD
+        return pl.ds(pl.multiple_of(at, D_HEAD), D_HEAD)
+
+    def remote(src, dst, send, recv, device):
+        return pltpu.make_async_remote_copy(
+            src_ref=src,
+            dst_ref=dst,
+            send_sem=send,
+            recv_sem=recv,
+            device_id={"ctx": device},
+            device_id_type=MESH,
+        )
+
+    def info_copy(offset):
+        return remote(
+            info_ref,
+            infos.at[me],
+            info_send.at[offset],
+            info_recv.at[offset],
+            partner(me, offset, n),
+        )
+
+    pairs = ((k_hbm, kr), (q_hbm, qr), (v_hbm, vr))
+
+    def qkv_copy(which, head, offset):
+        peer = partner(me, offset, n)
+        src, dst = pairs[which]
+        return remote(
+            src.at[:, head_of(peer, head)],
+            dst.at[head, rows_of(me)],
+            qkv_send.at[which, head, offset],
+            qkv_recv.at[which, head, offset],
+            peer,
+        )
+
+    def own_copy(which, head):
+        src, dst = pairs[which]
+        return pltpu.make_async_copy(
+            src.at[:, head_of(me, head)], dst.at[head, rows_of(me)], local_sem.at[which, head]
+        )
+
+    tail_copy = remote(
+        x_hbm.at[pl.ds(row_count - HALO, HALO)],
+        xb.at[pl.ds(0, HALO)],
+        halo_sem.at[0],
+        halo_sem.at[1],
+        (me + 1) % n,
+    )
+    above_copy = remote(
+        x_hbm.at[pl.ds(0, BLOCK)],
+        xb.at[pl.ds(HALO + row_count, BLOCK)],
+        halo_sem.at[2],
+        halo_sem.at[3],
+        (me + n - 1) % n,
+    )
+    own_rows = pltpu.make_async_copy(x_hbm, xb.at[pl.ds(HALO, row_count)], halo_sem.at[4])
+
+    for offset in order:
+        info_copy(offset).start()
+
+    @pl.when(me < n - 1)
+    def _():
+        tail_copy.start()
+
+    own_rows.start()
+    for head in range(head_count):
+        for which in range(3):
+            for offset in order:
+                qkv_copy(which, head, offset).start()
+            own_copy(which, head).start()
+
+    @pl.when(me > 0)
+    def _():
+        above_copy.start()
+
+    infos[me] = info_ref[...]
+    ob[:, pl.ds(seq_len, BLOCK), :] = jnp.zeros((head_count, BLOCK, D_HEAD), ob.dtype)
+    start_ref[pl.ds(seq_len, BLOCK), :] = jnp.zeros((BLOCK, LANES), jnp.int32)
+
+    @pl.when(me == 0)
+    def _():
+        xb[pl.ds(0, HALO), :] = jnp.zeros((HALO, channels), xb.dtype)
+
+    @pl.when(me == n - 1)
+    def _():
+        xb[pl.ds(HALO + row_count, BLOCK), :] = jnp.zeros((BLOCK, channels), xb.dtype)
+
+    for offset in order:
+        info_copy(offset).wait()
+
+    def bounds(device, carry):
+        for part in range(per_device):
+            segs = jnp.broadcast_to(infos[device, part : part + 1, :], (BLOCK, LANES)).T
+            reach = infos[device, per_device + part : per_device + part + 1, :]
+            count = jnp.zeros((BLOCK, LANES), jnp.float32)
+            for other in range(n):
+                for row in range(per_device):
+                    count = count + jnp.where(infos[other, row : row + 1, :] < segs, 1.0, 0.0)
+            begin = jnp.broadcast_to(
+                jnp.sum(count, axis=1, keepdims=True), (BLOCK, LANES)
+            ).astype(jnp.int32)
+            first = device * row_count + part * BLOCK
+            at = pl.ds(pl.multiple_of(first, BLOCK), BLOCK)
+            start_ref[at, :] = begin
+            lo_ref[at, :] = jnp.maximum(begin, first - reach)
+        return carry
+
+    lax.fori_loop(0, n, bounds, 0)
+
+    def convolve_block(block):
+        first = me * row_count + block * BLOCK
+        begin = start_ref[pl.ds(pl.multiple_of(first, BLOCK), BLOCK), :]
+        place = first + lax.broadcasted_iota(jnp.int32, (BLOCK, LANES), 0) - begin
+
+        def part(step, carry):
+            cols = pl.ds(pl.multiple_of(step * LANES, LANES), LANES)
+            rows = xb[pl.ds(block * BLOCK, BLOCK + HALO), cols].astype(jnp.float32)
+            running = jnp.broadcast_to(bias_ref[:, cols], (BLOCK, LANES))
+            for tap in range(KERNEL):
+                moved = rows if tap == 0 else pltpu.roll(rows, tap, 0)
+                moved = moved[HALO:]
+                if tap:
+                    moved = jnp.where(place >= tap, moved, 0.0)
+                running = running + weight_ref[tap : tap + 1, cols] * moved
+            gated = running / (1.0 + jnp.exp(-running))
+            conv_near[pl.ds(block * BLOCK, BLOCK), cols] = gated.astype(conv_near.dtype)
+            return carry
+
+        lax.fori_loop(0, channels // LANES, part, 0)
+
+    own_rows.wait()
+
+    @pl.when(me > 0)
+    def _():
+        tail_copy.wait_recv()
+
+    for block in range(per_device):
+        convolve_block(block)
+
+    def attend_rows(head, owner):
+        q = qr[head, rows_of(owner), :]
+        lo = lo_ref[rows_of(owner), :]
+        place = owner * row_count + lax.broadcasted_iota(jnp.int32, (row_count, LANES), 0)
+        lane = lax.broadcasted_iota(jnp.int32, (row_count, LANES), 1)
+        steps = (owner * row_count + row_count + chunk - 1) // chunk
+
+        def score(step, top):
+            keys = kr[head, pl.ds(pl.multiple_of(step * chunk, chunk), chunk), :]
+            scores = lax.dot_general(
+                q, keys, (((1,), (1,)), ((), ())), preferred_element_type=jnp.float32
+            )
+            for group in range(chunk // LANES):
+                at = step * chunk + group * LANES + lane
+                masked = jnp.where(
+                    (at >= lo) & (at <= place),
+                    scores[:, group * LANES : (group + 1) * LANES],
+                    masked_score,
+                )
+                s_ref[step, :, pl.ds(group * LANES, LANES)] = masked
+                top = jnp.maximum(top, masked)
+            return top
+
+        top = lax.fori_loop(
+            0, steps, score, jnp.full((row_count, LANES), masked_score, jnp.float32)
+        )
+        top = jnp.broadcast_to(jnp.max(top, axis=1, keepdims=True), (row_count, LANES))
+
+        def blend(step, carry):
+            total, mixed = carry
+            weights = []
+            for group in range(chunk // LANES):
+                scores = s_ref[step, :, pl.ds(group * LANES, LANES)]
+                lifted = jnp.exp2((scores - top) * scale)
+                total = total + lifted
+                weights.append(lifted.astype(jnp.bfloat16))
+            vals = vr[head, pl.ds(pl.multiple_of(step * chunk, chunk), chunk), :]
+            mixed = mixed + jnp.dot(
+                jnp.concatenate(weights, axis=1), vals, preferred_element_type=jnp.float32
+            )
+            return total, mixed
+
+        zero = jnp.zeros((row_count, LANES), jnp.float32)
+        total, mixed = lax.fori_loop(0, steps, blend, (zero, zero))
+        mixed = mixed / jnp.sum(total, axis=1, keepdims=True)
+        ob[head, rows_of(owner), :] = mixed.astype(ob.dtype)
+
+    def out_copy(head, offset):
+        peer = partner(me, offset, n)
+        return remote(
+            ob.at[head, rows_of(peer, near)],
+            attn_near.at[:, head_of(me, head)],
+            o_send.at[head, offset],
+            o_recv.at[head, offset],
+            peer,
+        )
+
+    def own_out(head):
+        return pltpu.make_async_copy(
+            ob.at[head, rows_of(me, near)], attn_near.at[:, head_of(me, head)], local_sem.at[3, head]
+        )
+
+    for head in range(head_count):
+        for which in range(3):
+            own_copy(which, head).wait()
+            for offset in order:
+                qkv_copy(which, head, offset).wait_recv()
+
+        def each(step, carry):
+            attend_rows(head, partner(me, (step + 2) % n, n))
+            return carry
+
+        lax.fori_loop(0, n, each, 0)
+        for offset in order:
+            out_copy(head, offset).start()
+        own_out(head).start()
+
+    @pl.when(me < n - 1)
+    def _():
+        above_copy.wait_recv()
+
+    convolve_block(per_device)
+
+    for head in range(head_count):
+        own_out(head).wait()
+        for offset in order:
+            out_copy(head, offset).wait()
+            for which in range(3):
+                qkv_copy(which, head, offset).wait_send()
+
+    @pl.when(me < n - 1)
+    def _():
+        tail_copy.wait_send()
+
+    @pl.when(me > 0)
+    def _():
+        above_copy.wait_send()
+
+
+def exchange(n, queries, key_rows, values, inner_rows, conv_weight, conv_bias, info):
+    row_count, features = queries.shape
+    channels = inner_rows.shape[1]
+    head_count = features // (n * D_HEAD)
+    seq_len = n * row_count
+    near = row_count + BLOCK
+    chunk = 2 * row_count if n % 2 == 0 else row_count
+    dtype = queries.dtype
+    hbm = pl.BlockSpec(memory_space=pl.ANY)
+    vmem = pl.BlockSpec(memory_space=pltpu.VMEM)
+    return pl.pallas_call(
+        functools.partial(exchange_kernel, n, row_count, head_count),
+        out_shape=(
+            jax.ShapeDtypeStruct((near, features), dtype),
+            jax.ShapeDtypeStruct((near, channels), dtype),
+        ),
+        in_specs=[hbm, hbm, hbm, hbm, vmem, vmem, vmem],
+        out_specs=(hbm, vmem),
+        scratch_shapes=[
+            pltpu.VMEM((head_count, seq_len, D_HEAD), dtype),
+            pltpu.VMEM((head_count, seq_len, D_HEAD), dtype),
+            pltpu.VMEM((head_count, seq_len, D_HEAD), dtype),
+            pltpu.VMEM((head_count, seq_len + BLOCK, D_HEAD), dtype),
+            pltpu.VMEM((HALO + near, channels), dtype),
+            pltpu.VMEM((n,) + info.shape, jnp.int32),
+            pltpu.VMEM((seq_len + BLOCK, LANES), jnp.int32),
+            pltpu.VMEM((seq_len, LANES), jnp.int32),
+            pltpu.VMEM((seq_len // chunk, row_count, chunk), jnp.float32),
+            pltpu.SemaphoreType.DMA((3, head_count, n)),
+            pltpu.SemaphoreType.DMA((3, head_count, n)),
+            pltpu.SemaphoreType.DMA((head_count, n)),
+            pltpu.SemaphoreType.DMA((head_count, n)),
+            pltpu.SemaphoreType.DMA((n,)),
+            pltpu.SemaphoreType.DMA((n,)),
+            pltpu.SemaphoreType.DMA((5,)),
+            pltpu.SemaphoreType.DMA((4, head_count)),
+        ],
+        compiler_params=pltpu.CompilerParams(
+            collective_id=0, has_side_effects=True, vmem_limit_bytes=56 * 1024 * 1024
+        ),
+    )(queries, key_rows, values, inner_rows, conv_weight, conv_bias, info)
+
+
+def by_heads(
+    queries,
+    key_rows,
+    values,
+    inner_rows,
+    conv_weight,
+    conv_bias,
+    segment_ids,
+    block_reach,
+    owner_counts,
+):
+    n = lax.axis_size("ctx")
+    here = lax.axis_index("ctx")
+    row_count = queries.shape[0]
+    per_device = row_count // BLOCK
+    near = row_count + BLOCK
+    info = jnp.concatenate(
+        [
+            segment_ids.reshape(per_device, BLOCK),
+            jnp.broadcast_to(block_reach[:, None], (per_device, BLOCK)),
+            jnp.zeros((-2 * per_device % 8, BLOCK), jnp.int32),
+        ],
+        axis=0,
+    )
+    attn_near, conv_near = exchange(
+        n, queries, key_rows, values, inner_rows, conv_weight, conv_bias[None, :], info
+    )
+    device = jnp.arange(n, dtype=jnp.int32)
+    first = jnp.sum(jnp.where(device < here, owner_counts, 0))
+    own = jnp.sum(jnp.where(device == here, owner_counts, 0))
+    moved = first > here * per_device
+    live = jnp.arange(near, dtype=jnp.int32) < own * BLOCK
+
+    def owned(rows):
+        shifted = jnp.pad(rows[BLOCK:], ((0, BLOCK), (0, 0)))
+        return jnp.where(live[:, None], jnp.where(moved, shifted, rows), 0)
+
+    return owned(attn_near), owned(conv_near)
+
+
+def plan(*args):
+    n = lax.axis_size("ctx")
+    row_count, features = args[0].shape
+    heads = features // D_HEAD
+    power = n > 2 and n & (n - 1) == 0
+    near_layout = row_count // BLOCK + (row_count // BLOCK) // 2 == row_count // BLOCK + 1
+    if power and near_layout and heads % n == 0 and n * row_count <= WINDOW:
+        return by_heads(*args)
+    return shards(*args)
+
+
 def solution(mesh):
     return jax.shard_map(
-        shards,
+        plan,
         mesh=mesh,
         in_specs=(
             P(("dp", "ctx"), None),

time: 385 us -> 84.9 us (0.22)
  the two profiles are of different devices: /device:TPU:1 before, /device:TPU:3 now
where the time goes in v1:
time: 84.9 us; the launch traced here: 84.6 us
  Pallas kernels  71.9 us (85%)
  other arithmetic  7.14 us (8%)
  local copies, waits for them, and re-layouts  3.61 us (4%)
  between operations  1.97 us (2%)
    pallas_call x1, Pallas kernels, exchange(): pl.pallas_call(functools.partial(exchange_kernel, n, row_count, head_coun...  71.9 us
    select_n x2, other arithmetic, owned(): return jnp.where(live[:, None], jnp.where(moved, shifted, rows), 0)  4.49 us

profile of v1, /device:TPU:3, one launch (start us, length us, event | category | flops | bytes accessed | tf_op | source)
XLA Modules:
  0.0 84.6 jit_solution(11004294883892606428)
XLA Ops:
  0.6 0.7 pad.11.clone
  1.4 0.1 pad.12.clone
  1.4 1.3 %fusion.1 = (s32[]{:T(128)}, s32[]{:T(128)}) fusion(s32[8]{0:T(128)} %param.17, s32[]{:T(128)S(6)} %axis_index.12), kind=kLoop, calls=%fused_computation.7 | loop fusion | flops 46 | bytes 44 | tf_op jit(solution)/shard_map/reduce_sum | solution.py:513
  4.1 1.3 %add_add_fusion.info_ref = s32[8,128]{1,0:T(8,128)} fusion(s32[2,128]{1,0:T(2,128)} %bitcast.3, s32[8]{0:T(128)S(1)} %pad.12.clone, s32[8]{0:T(128)S(1)} %pad.11.clone), kind=kLoop, calls=%fused_computation.2 | loop fusion | flops 2048 | bytes 5184 | tf_op jit(solution)/shard_map/concatenate | solution.py:501
  5.4 71.9 %shard_map.104 = (bf16[384,2048]{1,0:T(8,128)(2,1)}, bf16[384,4096]{1,0:T(8,128)(2,1)}) custom-call(bf16[256,2048]{1,0:T(8,128)(2,1)} %q_hbm.1, bf16[256,2048]{1,0:T(8,128)(2,1)} %k_hbm.1, bf16[256,2048]{1,0:T(8,128)(2,1)} %v_hbm.1, bf16[256,4096]{1,0:T(8,128)(2,1)} %x_hbm.1, f32[4,4096]{1,0:T(4,128)} %weight_ref.1, f32[1,4096]{1,0:T(1,128)} %bitcast.2, ...), custom_call_target="tpu_custom_call" | custom-call | tf_op jit(solution)/shard_map/pallas_call | solution.py:452
  77.3 0.0 copy-start.1
  77.3 1.4 %slice.6 = bf16[256,2048]{1,0:T(8,128)(2,1)S(1)} slice(bf16[384,2048]{1,0:T(8,128)(2,1)} %get-tuple-element.4), slice={[128:384], [0:2048]} | slice | bytes 2097152 | tf_op jit(solution)/shard_map/slice | solution.py:519
  78.7 0.3 copy-done.1
  79.0 0.0 copy-start
  79.0 1.6 %select_select_fusion.1 = bf16[384,2048]{1,0:T(8,128)(2,1)} fusion(bf16[384,2048]{1,0:T(8,128)(2,1)S(1)} %copy-done.1, bf16[256,2048]{1,0:T(8,128)(2,1)S(1)} %slice.6, pred[384]{0:T(512)(128)(4,1)S(1)} %iota_compare_fusion, pred[]{:T(512)S(6)} %gt.3), kind=kLoop, calls=%fused_computation.1 | loop fusion | flops 1572864 | bytes 4194689 | tf_op jit(solution)/shard_map/jit(_where)/select_n | solution.py:520
  80.6 0.9 %copy-done = bf16[384,4096]{1,0:T(8,128)(2,1)S(1)} copy-done((bf16[384,4096]{1,0:T(8,128)(2,1)S(1)}, bf16[384,4096]{1,0:T(8,128)(2,1)}, u32[]{:S(2)}) %copy-start) | copy-done | bytes 3145752
  81.5 0.2 slice.7
  81.7 2.9 %select_select_fusion = bf16[384,4096]{1,0:T(8,128)(2,1)} fusion(bf16[384,4096]{1,0:T(8,128)(2,1)S(1)} %copy-done, bf16[256,4096]{1,0:T(8,128)(2,1)S(1)} %slice.7, pred[384]{0:T(512)(128)(4,1)S(1)} %iota_compare_fusion, pred[]{:T(512)S(6)} %gt.3), kind=kLoop, calls=%fused_computation | loop fusion | flops 3145728 | bytes 8388993 | tf_op jit(solution)/shard_map/jit(_where)/select_n | solution.py:520
  (2 shorter events, 0.0 us)
Async XLA Ops:
  77.3 1.7 %copy-start.1 = (bf16[384,2048]{1,0:T(8,128)(2,1)S(1)}, bf16[384,2048]{1,0:T(8,128)(2,1)}, u32[]{:S(2)}) copy-start(bf16[384,2048]{1,0:T(8,128)(2,1)} %get-tuple-element.4) | copy-start | bytes 4718596
  79.0 2.5 %copy-start = (bf16[384,4096]{1,0:T(8,128)(2,1)S(1)}, bf16[384,4096]{1,0:T(8,128)(2,1)}, u32[]{:S(2)}) copy-start(bf16[384,4096]{1,0:T(8,128)(2,1)} %get-tuple-element.5) | copy-start | bytes 9437188

commit v2 on v1

--- a/solution.py
+++ b/solution.py
@@ -139,6 +139,7 @@
 
 LANES = 128
 HALO = 16
+PAIR = 2
 MESH = pl.DeviceIdType.MESH
 
 
@@ -168,6 +169,11 @@
     vr,
     ob,
     xb,
+    conv_buf,
+    q_full,
+    k_full,
+    v_full,
+    o_full,
     infos,
     start_ref,
     lo_ref,
@@ -176,6 +182,11 @@
     qkv_recv,
     o_send,
     o_recv,
+    extra_send,
+    extra_recv,
+    pass_send,
+    pass_recv,
+    full_sem,
     info_send,
     info_recv,
     halo_sem,
@@ -183,7 +194,6 @@
 ):
     me = lax.axis_index("ctx")
     per_device = row_count // BLOCK
-    near = row_count + BLOCK
     seq_len = n * row_count
     channels = bias_ref.shape[1]
     chunk = s_ref.shape[2]
@@ -256,6 +266,25 @@
         halo_sem.at[3],
         (me + n - 1) % n,
     )
+    full_copies = [
+        pltpu.make_async_copy(q_hbm, q_full, full_sem.at[0]),
+        pltpu.make_async_copy(k_hbm, k_full.at[rows_of(me % PAIR)], full_sem.at[1]),
+        pltpu.make_async_copy(v_hbm, v_full.at[rows_of(me % PAIR)], full_sem.at[2]),
+    ]
+    pair_copies = [
+        remote(
+            src,
+            dst.at[pl.ds(0, row_count)],
+            full_sem.at[3 + 2 * i],
+            full_sem.at[4 + 2 * i],
+            partner(me, 1, n),
+        )
+        for i, (src, dst) in enumerate(((k_hbm, k_full), (v_hbm, v_full)))
+    ]
+
+    def sends(which, device):
+        return device >= (PAIR if which == 1 else 0)
+
     own_rows = pltpu.make_async_copy(x_hbm, xb.at[pl.ds(HALO, row_count)], halo_sem.at[4])
 
     for offset in order:
@@ -266,10 +295,24 @@
         tail_copy.start()
 
     own_rows.start()
+    @pl.when(me < PAIR)
+    def _():
+        for copy in full_copies:
+            copy.start()
+
+    @pl.when(me == 0)
+    def _():
+        for copy in pair_copies:
+            copy.start()
+
     for head in range(head_count):
         for which in range(3):
             for offset in order:
-                qkv_copy(which, head, offset).start()
+
+                @pl.when(sends(which, me))
+                def _():
+                    qkv_copy(which, head, offset).start()
+
             own_copy(which, head).start()
 
     @pl.when(me > 0)
@@ -277,12 +320,12 @@
         above_copy.start()
 
     infos[me] = info_ref[...]
-    ob[:, pl.ds(seq_len, BLOCK), :] = jnp.zeros((head_count, BLOCK, D_HEAD), ob.dtype)
     start_ref[pl.ds(seq_len, BLOCK), :] = jnp.zeros((BLOCK, LANES), jnp.int32)
 
     @pl.when(me == 0)
     def _():
         xb[pl.ds(0, HALO), :] = jnp.zeros((HALO, channels), xb.dtype)
+        v_full[pl.ds(row_count, row_count), :] = jnp.zeros(q_full.shape, v_full.dtype)
 
     @pl.when(me == n - 1)
     def _():
@@ -326,7 +369,7 @@
                     moved = jnp.where(place >= tap, moved, 0.0)
                 running = running + weight_ref[tap : tap + 1, cols] * moved
             gated = running / (1.0 + jnp.exp(-running))
-            conv_near[pl.ds(block * BLOCK, BLOCK), cols] = gated.astype(conv_near.dtype)
+            conv_buf[pl.ds(block * BLOCK, BLOCK), cols] = gated.astype(conv_buf.dtype)
             return carry
 
         lax.fori_loop(0, channels // LANES, part, 0)
@@ -340,15 +383,20 @@
     for block in range(per_device):
         convolve_block(block)
 
-    def attend_rows(head, owner):
-        q = qr[head, rows_of(owner), :]
+    def conv_out(at, count, sem):
+        rows = pl.ds(at, count)
+        return pltpu.make_async_copy(conv_buf.at[rows], conv_near.at[rows], halo_sem.at[sem])
+
+    conv_out(0, row_count, 5).start()
+
+    def attend_rows(q, keys_at, values_at, owner):
         lo = lo_ref[rows_of(owner), :]
         place = owner * row_count + lax.broadcasted_iota(jnp.int32, (row_count, LANES), 0)
         lane = lax.broadcasted_iota(jnp.int32, (row_count, LANES), 1)
         steps = (owner * row_count + row_count + chunk - 1) // chunk
 
         def score(step, top):
-            keys = kr[head, pl.ds(pl.multiple_of(step * chunk, chunk), chunk), :]
+            keys = keys_at(pl.ds(pl.multiple_of(step * chunk, chunk), chunk))
             scores = lax.dot_general(
                 q, keys, (((1,), (1,)), ((), ())), preferred_element_type=jnp.float32
             )
@@ -376,7 +424,7 @@
                 lifted = jnp.exp2((scores - top) * scale)
                 total = total + lifted
                 weights.append(lifted.astype(jnp.bfloat16))
-            vals = vr[head, pl.ds(pl.multiple_of(step * chunk, chunk), chunk), :]
+            vals = values_at(pl.ds(pl.multiple_of(step * chunk, chunk), chunk))
             mixed = mixed + jnp.dot(
                 jnp.concatenate(weights, axis=1), vals, preferred_element_type=jnp.float32
             )
@@ -385,50 +433,192 @@
         zero = jnp.zeros((row_count, LANES), jnp.float32)
         total, mixed = lax.fori_loop(0, steps, blend, (zero, zero))
         mixed = mixed / jnp.sum(total, axis=1, keepdims=True)
-        ob[head, rows_of(owner), :] = mixed.astype(ob.dtype)
+        return mixed.astype(jnp.bfloat16)
+
+    own_rows_at = pl.ds(0, row_count)
+    extra_at = pl.ds(row_count, BLOCK)
+    full_out = pltpu.make_async_copy(o_full, attn_near.at[own_rows_at], full_sem.at[7])
+
+    @pl.when(me < PAIR)
+    def _():
+        for copy in full_copies:
+            copy.wait()
+
+        @pl.when(me == 1)
+        def _():
+            for copy in pair_copies:
+                copy.wait_recv()
+
+        def each(head, carry):
+            cols = pl.ds(pl.multiple_of(head * D_HEAD, D_HEAD), D_HEAD)
+            o_full[:, cols] = attend_rows(
+                q_full[:, cols], lambda at: k_full[at, cols], lambda at: v_full[at, cols], me
+            )
+            return carry
+
+        lax.fori_loop(0, n * head_count, each, 0)
+        full_out.start()
 
     def out_copy(head, offset):
         peer = partner(me, offset, n)
         return remote(
-            ob.at[head, rows_of(peer, near)],
-            attn_near.at[:, head_of(me, head)],
+            ob.at[head, rows_of(peer)],
+            attn_near.at[own_rows_at, head_of(me, head)],
             o_send.at[head, offset],
             o_recv.at[head, offset],
             peer,
         )
 
+    def extra_copy(head, offset):
+        peer = partner(me, offset, n)
+        return remote(
+            ob.at[head, rows_of((peer + 1) % n, BLOCK)],
+            attn_near.at[extra_at, head_of(me, head)],
+            extra_send.at[head, offset],
+            extra_recv.at[head, offset],
+            peer,
+        )
+
     def own_out(head):
         return pltpu.make_async_copy(
-            ob.at[head, rows_of(me, near)], attn_near.at[:, head_of(me, head)], local_sem.at[3, head]
-        )
+            ob.at[head, rows_of(me)],
+            attn_near.at[own_rows_at, head_of(me, head)],
+            local_sem.at[3, head],
+        )
+
+    def own_extra(head):
+        return pltpu.make_async_copy(
+            ob.at[head, rows_of((me + 1) % n, BLOCK)],
+            attn_near.at[extra_at, head_of(me, head)],
+            local_sem.at[4, head],
+        )
+
+    def pass_copy(offset):
+        at = partner(me, offset, n) * (head_count * D_HEAD)
+        cols = pl.ds(pl.multiple_of(at, D_HEAD), head_count * D_HEAD)
+        return remote(
+            attn_near.at[pl.ds(0, BLOCK), cols],
+            attn_near.at[extra_at, cols],
+            pass_send.at[offset],
+            pass_recv.at[offset],
+            partner(me, 1, n),
+        )
+
+    def far(device):
+        return device >= PAIR
+
+    def extra(device):
+        return (device % PAIR == PAIR - 1) & (device < n - 1)
+
+    odd = me % PAIR == PAIR - 1
 
     for head in range(head_count):
         for which in range(3):
             own_copy(which, head).wait()
             for offset in order:
-                qkv_copy(which, head, offset).wait_recv()
+
+                @pl.when(sends(which, partner(me, offset, n)))
+                def _():
+                    qkv_copy(which, head, offset).wait_recv()
 
         def each(step, carry):
-            attend_rows(head, partner(me, (step + 2) % n, n))
+            owner = partner(me, (step + 2) % n, n)
+
+            @pl.when(far(owner))
+            def _():
+                ob[head, rows_of(owner), :] = attend_rows(
+                    qr[head, rows_of(owner), :],
+                    lambda at: kr[head, at, :],
+                    lambda at: vr[head, at, :],
+                    owner,
+                )
+
             return carry
 
         lax.fori_loop(0, n, each, 0)
         for offset in order:
-            out_copy(head, offset).start()
-        own_out(head).start()
+            peer = partner(me, offset, n)
+
+            @pl.when(far(peer))
+            def _():
+                out_copy(head, offset).start()
+
+            @pl.when(extra(peer))
+            def _():
+                extra_copy(head, offset).start()
+
+        @pl.when(far(me))
+        def _():
+            own_out(head).start()
+
+        @pl.when(extra(me))
+        def _():
+            own_extra(head).start()
 
     @pl.when(me < n - 1)
     def _():
         above_copy.wait_recv()
 
     convolve_block(per_device)
+    conv_out(row_count, BLOCK, 6).start()
+
+    @pl.when(me < PAIR)
+    def _():
+        full_out.wait()
+
+    for offset in [0] + order:
+
+        @pl.when(far(me))
+        def _():
+            for head in range(head_count):
+                if offset:
+                    out_copy(head, offset).wait_recv()
+                else:
+                    own_out(head).wait()
+
+        @pl.when(odd)
+        def _():
+            pass_copy(offset).start()
+
+    @pl.when(extra(me))
+    def _():
+        for head in range(head_count):
+            own_extra(head).wait()
+            for offset in order:
+                extra_copy(head, offset).wait_recv()
+
+    for offset in [0] + order:
+
+        @pl.when(odd)
+        def _():
+            pass_copy(offset).wait_send()
+
+        @pl.when(jnp.logical_not(odd))
+        def _():
+            pass_copy(offset).wait_recv()
 
     for head in range(head_count):
-        own_out(head).wait()
         for offset in order:
-            out_copy(head, offset).wait()
+            peer = partner(me, offset, n)
+
+            @pl.when(far(peer))
+            def _():
+                out_copy(head, offset).wait_send()
+
+            @pl.when(extra(peer))
+            def _():
+                extra_copy(head, offset).wait_send()
+
             for which in range(3):
-                qkv_copy(which, head, offset).wait_send()
+
+                @pl.when(sends(which, me))
+                def _():
+                    qkv_copy(which, head, offset).wait_send()
+
+    @pl.when(me == 0)
+    def _():
+        for copy in pair_copies:
+            copy.wait_send()
 
     @pl.when(me < n - 1)
     def _():
@@ -437,6 +627,9 @@
     @pl.when(me > 0)
     def _():
         above_copy.wait_send()
+
+    conv_out(0, row_count, 5).wait()
+    conv_out(row_count, BLOCK, 6).wait()
 
 
 def exchange(n, queries, key_rows, values, inner_rows, conv_weight, conv_bias, info):
@@ -445,7 +638,7 @@
     head_count = features // (n * D_HEAD)
     seq_len = n * row_count
     near = row_count + BLOCK
-    chunk = 2 * row_count if n % 2 == 0 else row_count
+    chunk = PAIR * row_count
     dtype = queries.dtype
     hbm = pl.BlockSpec(memory_space=pl.ANY)
     vmem = pl.BlockSpec(memory_space=pltpu.VMEM)
@@ -456,13 +649,18 @@
             jax.ShapeDtypeStruct((near, channels), dtype),
         ),
         in_specs=[hbm, hbm, hbm, hbm, vmem, vmem, vmem],
-        out_specs=(hbm, vmem),
+        out_specs=(hbm, hbm),
         scratch_shapes=[
             pltpu.VMEM((head_count, seq_len, D_HEAD), dtype),
             pltpu.VMEM((head_count, seq_len, D_HEAD), dtype),
             pltpu.VMEM((head_count, seq_len, D_HEAD), dtype),
-            pltpu.VMEM((head_count, seq_len + BLOCK, D_HEAD), dtype),
+            pltpu.VMEM((head_count, seq_len, D_HEAD), dtype),
             pltpu.VMEM((HALO + near, channels), dtype),
+            pltpu.VMEM((near, channels), dtype),
+            pltpu.VMEM((row_count, features), dtype),
+            pltpu.VMEM((chunk, features), dtype),
+            pltpu.VMEM((chunk, features), dtype),
+            pltpu.VMEM((row_count, features), dtype),
             pltpu.VMEM((n,) + info.shape, jnp.int32),
             pltpu.VMEM((seq_len + BLOCK, LANES), jnp.int32),
             pltpu.VMEM((seq_len, LANES), jnp.int32),
@@ -471,15 +669,63 @@
             pltpu.SemaphoreType.DMA((3, head_count, n)),
             pltpu.SemaphoreType.DMA((head_count, n)),
             pltpu.SemaphoreType.DMA((head_count, n)),
+            pltpu.SemaphoreType.DMA((head_count, n)),
+            pltpu.SemaphoreType.DMA((head_count, n)),
             pltpu.SemaphoreType.DMA((n,)),
             pltpu.SemaphoreType.DMA((n,)),
-            pltpu.SemaphoreType.DMA((5,)),
-            pltpu.SemaphoreType.DMA((4, head_count)),
+            pltpu.SemaphoreType.DMA((8,)),
+            pltpu.SemaphoreType.DMA((n,)),
+            pltpu.SemaphoreType.DMA((n,)),
+            pltpu.SemaphoreType.DMA((7,)),
+            pltpu.SemaphoreType.DMA((5, head_count)),
         ],
         compiler_params=pltpu.CompilerParams(
             collective_id=0, has_side_effects=True, vmem_limit_bytes=56 * 1024 * 1024
         ),
     )(queries, key_rows, values, inner_rows, conv_weight, conv_bias, info)
+
+
+def owned_kernel(counts_ref, here_ref, attn_ref, conv_ref, attn_out, conv_out, *, steps):
+    own = counts_ref[here_ref[0]] * steps
+    live = pl.program_id(0) < own
+
+    @pl.when(live)
+    def _():
+        attn_out[...] = attn_ref[...]
+        conv_out[...] = conv_ref[...]
+
+    @pl.when(jnp.logical_not(live))
+    def _():
+        attn_out[...] = jnp.zeros_like(attn_out)
+        conv_out[...] = jnp.zeros_like(conv_out)
+
+
+def owned(n, per_device, owner_counts, here, attn_near, conv_near):
+    near = attn_near.shape[0]
+    steps = 2
+    rows = BLOCK // steps
+    last = near // rows - 1
+
+    def source(i, counts, here):
+        first = 0
+        for device in range(n):
+            first = first + jnp.where(device < here[0], counts[device], 0)
+        moved = first - here[0] * per_device
+        return (jnp.minimum(i + moved * steps, last), 0)
+
+    shapes = (attn_near, conv_near)
+    return pl.pallas_call(
+        functools.partial(owned_kernel, steps=steps),
+        out_shape=tuple(jax.ShapeDtypeStruct(a.shape, a.dtype) for a in shapes),
+        grid_spec=pltpu.PrefetchScalarGridSpec(
+            num_scalar_prefetch=2,
+            grid=(near // rows,),
+            in_specs=[pl.BlockSpec((rows, a.shape[1]), source) for a in shapes],
+            out_specs=tuple(
+                pl.BlockSpec((rows, a.shape[1]), lambda i, counts, here: (i, 0)) for a in shapes
+            ),
+        ),
+    )(owner_counts, here[None], attn_near, conv_near)
 
 
 def by_heads(
@@ -497,7 +743,6 @@
     here = lax.axis_index("ctx")
     row_count = queries.shape[0]
     per_device = row_count // BLOCK
-    near = row_count + BLOCK
     info = jnp.concatenate(
         [
             segment_ids.reshape(per_device, BLOCK),
@@ -509,17 +754,7 @@
     attn_near, conv_near = exchange(
         n, queries, key_rows, values, inner_rows, conv_weight, conv_bias[None, :], info
     )
-    device = jnp.arange(n, dtype=jnp.int32)
-    first = jnp.sum(jnp.where(device < here, owner_counts, 0))
-    own = jnp.sum(jnp.where(device == here, owner_counts, 0))
-    moved = first > here * per_device
-    live = jnp.arange(near, dtype=jnp.int32) < own * BLOCK
-
-    def owned(rows):
-        shifted = jnp.pad(rows[BLOCK:], ((0, BLOCK), (0, 0)))
-        return jnp.where(live[:, None], jnp.where(moved, shifted, rows), 0)
-
-    return owned(attn_near), owned(conv_near)
+    return owned(n, per_device, owner_counts, here, attn_near, conv_near)
 
 
 def plan(*args):

time: 84.9 us -> 77.3 us (0.910); the launches traced: 84.6 us -> 76.1 us
  other arithmetic: 7.14 us -> 1.34 us
  local copies, waits for them, and re-layouts: 3.61 us -> 0.81 us
  Pallas kernels: 71.9 us -> 73.3 us
  between operations: 1.97 us -> 0.64 us
    pallas_call x0 -> x1, Pallas kernels: none -> 5.79 us  [owned(): pl.pallas_call(functools.partial(owned_kernel, steps=steps), out_shape=tu...]
    select_n x2 -> x0, other arithmetic: 4.49 us -> none  [owned(): return jnp.where(live[:, None], jnp.where(moved, shifted, rows), 0)]
    pallas_call x1, Pallas kernels: 71.9 us -> 67.6 us  [exchange(): pl.pallas_call(functools.partial(exchange_kernel, n, row_count, head_coun...]
    slice x2 -> x0, local copies, waits for them, and re-layouts: 1.62 us -> none  [owned(): shifted = jnp.pad(rows[BLOCK:], ((0, BLOCK), (0, 0)))]
    reduce_sum x1 -> x0, other arithmetic: 1.3 us -> none  [by_heads(): first = jnp.sum(jnp.where(device < here, owner_counts, 0))]
    unnamed x4 -> x0, local copies, waits for them, and re-layouts: 1.18 us -> none
where the time goes in v2:
time: 77.3 us; the launch traced here: 76.1 us
  Pallas kernels  73.3 us (95%)
  other arithmetic  1.34 us (2%)
  local copies, waits for them, and re-layouts  0.81 us (1%)
    pallas_call x1, Pallas kernels, exchange(): pl.pallas_call(functools.partial(exchange_kernel, n, row_count, head_coun...  67.6 us
    pallas_call x1, Pallas kernels, owned(): pl.pallas_call(functools.partial(owned_kernel, steps=steps), out_shape=tu...  5.79 us

profile of v2, /device:TPU:3, one launch (start us, length us, event | category | flops | bytes accessed | tf_op | source)
XLA Modules:
  0.0 76.1 jit_solution(1892848152448540419)
XLA Ops:
  0.6 0.7 pad.1.clone
  1.4 0.1 pad.2.clone
  1.4 1.3 %add_add_fusion.info_ref = s32[8,128]{1,0:T(8,128)} fusion(s32[2,128]{1,0:T(2,128)} %bitcast.4, s32[8]{0:T(128)S(1)} %pad.2.clone, s32[8]{0:T(128)S(1)} %pad.1.clone), kind=kLoop, calls=%fused_computation | loop fusion | flops 2048 | bytes 5184 | tf_op jit(solution)/shard_map/concatenate | solution.py:746
  2.8 67.6 %shard_map.104 = (bf16[384,2048]{1,0:T(8,128)(2,1)}, bf16[384,4096]{1,0:T(8,128)(2,1)}) custom-call(bf16[256,2048]{1,0:T(8,128)(2,1)} %q_hbm.1, bf16[256,2048]{1,0:T(8,128)(2,1)} %k_hbm.1, bf16[256,2048]{1,0:T(8,128)(2,1)} %v_hbm.1, bf16[256,4096]{1,0:T(8,128)(2,1)} %x_hbm.1, f32[4,4096]{1,0:T(4,128)} %weight_ref.1, f32[1,4096]{1,0:T(1,128)} %bitcast.3, ...), custom_call_target="tpu_custom_call" | custom-call | tf_op jit(solution)/shard_map/pallas_call | solution.py:645
  70.3 5.8 %shard_map.105 = (bf16[384,2048]{1,0:T(8,128)(2,1)}, bf16[384,4096]{1,0:T(8,128)(2,1)}) custom-call(s32[8]{0:T(128)} %counts_ref.1, s32[1]{0:T(128)} %bitcast.here_ref, bf16[384,2048]{1,0:T(8,128)(2,1)} %get-tuple-element.4.attn_ref, bf16[384,4096]{1,0:T(8,128)(2,1)} %get-tuple-element.5.conv_ref), custom_call_target="tpu_custom_call" | custom-call | tf_op jit(solution)/shard_map/pallas_call | solution.py:717
  (1 shorter events, 0.0 us)

commit v3 on v2

--- a/solution.py
+++ b/solution.py
@@ -161,7 +161,8 @@
     x_hbm,
     weight_ref,
     bias_ref,
-    info_ref,
+    segment_ref,
+    reach_ref,
     attn_near,
     conv_near,
     qr,
@@ -174,6 +175,7 @@
     k_full,
     v_full,
     o_full,
+    info_ref,
     infos,
     start_ref,
     lo_ref,
@@ -200,6 +202,13 @@
     scale = math.log2(math.e) / math.sqrt(D_HEAD)
     order = list(range(2, n)) + [1]
 
+    info_ref[...] = jnp.zeros_like(info_ref)
+    info_ref[pl.ds(0, per_device), :] = segment_ref[...]
+    for part in range(per_device):
+        info_ref[per_device + part : per_device + part + 1, :] = jnp.full(
+            (1, LANES), reach_ref[part], jnp.int32
+        )
+
     barrier = pltpu.get_barrier_semaphore()
     for offset in range(1, n):
         pl.semaphore_signal(
@@ -632,13 +641,16 @@
     conv_out(row_count, BLOCK, 6).wait()
 
 
-def exchange(n, queries, key_rows, values, inner_rows, conv_weight, conv_bias, info):
+def exchange(
+    n, queries, key_rows, values, inner_rows, conv_weight, conv_bias, segments, block_reach
+):
     row_count, features = queries.shape
     channels = inner_rows.shape[1]
     head_count = features // (n * D_HEAD)
     seq_len = n * row_count
     near = row_count + BLOCK
     chunk = PAIR * row_count
+    info_rows = pl.cdiv(2 * segments.shape[0], 8) * 8
     dtype = queries.dtype
     hbm = pl.BlockSpec(memory_space=pl.ANY)
     vmem = pl.BlockSpec(memory_space=pltpu.VMEM)
@@ -648,7 +660,7 @@
             jax.ShapeDtypeStruct((near, features), dtype),
             jax.ShapeDtypeStruct((near, channels), dtype),
         ),
-        in_specs=[hbm, hbm, hbm, hbm, vmem, vmem, vmem],
+        in_specs=[hbm, hbm, hbm, hbm, vmem, vmem, vmem, pl.BlockSpec(memory_space=pltpu.SMEM)],
         out_specs=(hbm, hbm),
         scratch_shapes=[
             pltpu.VMEM((head_count, seq_len, D_HEAD), dtype),
@@ -661,7 +673,8 @@
             pltpu.VMEM((chunk, features), dtype),
             pltpu.VMEM((chunk, features), dtype),
             pltpu.VMEM((row_count, features), dtype),
-            pltpu.VMEM((n,) + info.shape, jnp.int32),
+            pltpu.VMEM((info_rows, LANES), jnp.int32),
+            pltpu.VMEM((n, info_rows, LANES), jnp.int32),
             pltpu.VMEM((seq_len + BLOCK, LANES), jnp.int32),
             pltpu.VMEM((seq_len, LANES), jnp.int32),
             pltpu.VMEM((seq_len // chunk, row_count, chunk), jnp.float32),
@@ -682,50 +695,78 @@
         compiler_params=pltpu.CompilerParams(
             collective_id=0, has_side_effects=True, vmem_limit_bytes=56 * 1024 * 1024
         ),
-    )(queries, key_rows, values, inner_rows, conv_weight, conv_bias, info)
-
-
-def owned_kernel(counts_ref, here_ref, attn_ref, conv_ref, attn_out, conv_out, *, steps):
-    own = counts_ref[here_ref[0]] * steps
-    live = pl.program_id(0) < own
-
-    @pl.when(live)
-    def _():
-        attn_out[...] = attn_ref[...]
-        conv_out[...] = conv_ref[...]
-
-    @pl.when(jnp.logical_not(live))
-    def _():
-        attn_out[...] = jnp.zeros_like(attn_out)
-        conv_out[...] = jnp.zeros_like(conv_out)
-
-
-def owned(n, per_device, owner_counts, here, attn_near, conv_near):
+    )(queries, key_rows, values, inner_rows, conv_weight, conv_bias, segments, block_reach)
+
+
+def owned_kernel(
+    n, per_device, counts_ref, attn_near, conv_near, attn_out, conv_out, attn_buf, conv_buf, zero, sems
+):
+    here = lax.axis_index("ctx")
+    first = 0
+    for device in range(n):
+        first = first + jnp.where(device < here, counts_ref[device], 0)
+    moved = jnp.clip(first - here * per_device, 0, 1)
+    own = counts_ref[here]
+    blocks = attn_near.shape[0] // BLOCK
+    trios = ((attn_near, attn_buf, attn_out), (conv_near, conv_buf, conv_out))
+
+    def fetch(block, which):
+        src, buf, _ = trios[which]
+        at = pl.multiple_of(jnp.minimum(block + moved, blocks - 1) * BLOCK, BLOCK)
+        return pltpu.make_async_copy(
+            src.at[pl.ds(at, BLOCK)], buf.at[block], sems.at[0, which, block]
+        )
+
+    def store(block, which, source):
+        dst = trios[which][2]
+        return pltpu.make_async_copy(
+            source, dst.at[pl.ds(block * BLOCK, BLOCK)], sems.at[1, which, block]
+        )
+
+    for block in range(blocks):
+
+        @pl.when(block < own)
+        def _():
+            for which in range(2):
+                fetch(block, which).start()
+
+    zero[...] = jnp.zeros_like(zero)
+    for block in range(blocks):
+
+        @pl.when(block < own)
+        def _():
+            for which in range(2):
+                fetch(block, which).wait()
+                store(block, which, trios[which][1].at[block]).start()
+
+        @pl.when(block >= own)
+        def _():
+            for which in range(2):
+                width = trios[which][0].shape[1]
+                store(block, which, zero.at[:, pl.ds(0, width)]).start()
+
+    for block in range(blocks):
+        for which in range(2):
+            store(block, which, trios[which][1].at[block]).wait()
+
+
+def owned(n, per_device, owner_counts, attn_near, conv_near):
     near = attn_near.shape[0]
-    steps = 2
-    rows = BLOCK // steps
-    last = near // rows - 1
-
-    def source(i, counts, here):
-        first = 0
-        for device in range(n):
-            first = first + jnp.where(device < here[0], counts[device], 0)
-        moved = first - here[0] * per_device
-        return (jnp.minimum(i + moved * steps, last), 0)
-
-    shapes = (attn_near, conv_near)
+    blocks = near // BLOCK
+    widths = [a.shape[1] for a in (attn_near, conv_near)]
+    hbm = pl.BlockSpec(memory_space=pl.ANY)
     return pl.pallas_call(
-        functools.partial(owned_kernel, steps=steps),
-        out_shape=tuple(jax.ShapeDtypeStruct(a.shape, a.dtype) for a in shapes),
-        grid_spec=pltpu.PrefetchScalarGridSpec(
-            num_scalar_prefetch=2,
-            grid=(near // rows,),
-            in_specs=[pl.BlockSpec((rows, a.shape[1]), source) for a in shapes],
-            out_specs=tuple(
-                pl.BlockSpec((rows, a.shape[1]), lambda i, counts, here: (i, 0)) for a in shapes
-            ),
-        ),
-    )(owner_counts, here[None], attn_near, conv_near)
+        functools.partial(owned_kernel, n, per_device),
+        out_shape=tuple(jax.ShapeDtypeStruct(a.shape, a.dtype) for a in (attn_near, conv_near)),
+        in_specs=[pl.BlockSpec(memory_space=pltpu.SMEM), hbm, hbm],
+        out_specs=(hbm, hbm),
+        scratch_shapes=[
+            pltpu.VMEM((blocks, BLOCK, widths[0]), attn_near.dtype),
+            pltpu.VMEM((blocks, BLOCK, widths[1]), conv_near.dtype),
+            pltpu.VMEM((BLOCK, max(widths)), attn_near.dtype),
+            pltpu.SemaphoreType.DMA((2, 2, blocks)),
+        ],
+    )(owner_counts, attn_near, conv_near)
 
 
 def by_heads(
@@ -740,21 +781,20 @@
     owner_counts,
 ):
     n = lax.axis_size("ctx")
-    here = lax.axis_index("ctx")
     row_count = queries.shape[0]
     per_device = row_count // BLOCK
-    info = jnp.concatenate(
-        [
-            segment_ids.reshape(per_device, BLOCK),
-            jnp.broadcast_to(block_reach[:, None], (per_device, BLOCK)),
-            jnp.zeros((-2 * per_device % 8, BLOCK), jnp.int32),
-        ],
-        axis=0,
-    )
     attn_near, conv_near = exchange(
-        n, queries, key_rows, values, inner_rows, conv_weight, conv_bias[None, :], info
-    )
-    return owned(n, per_device, owner_counts, here, attn_near, conv_near)
+        n,
+        queries,
+        key_rows,
+        values,
+        inner_rows,
+        conv_weight,
+        conv_bias[None, :],
+        segment_ids.reshape(per_device, BLOCK),
+        block_reach,
+    )
+    return owned(n, per_device, owner_counts, attn_near, conv_near)
 
 
 def plan(*args):

time: 77.3 us -> 73.2 us (0.947)
  Pallas kernels: 73.3 us -> 71.8 us
  other arithmetic: 1.34 us -> 0 us
  local copies, waits for them, and re-layouts: 0.81 us -> 0 us
    pallas_call x1, Pallas kernels: 5.79 us -> 4.18 us  [owned(): pl.pallas_call(functools.partial(owned_kernel, n, per_device), out_shape=...]
    concatenate x1 -> x0, other arithmetic: 1.34 us -> none  [by_heads(): jnp.concatenate([segment_ids.reshape(per_device, BLOCK), jnp.broadcast_to...]
    concatenate x2 -> x0, local copies, waits for them, and re-layouts: 0.81 us -> none  [by_heads(): jnp.concatenate([segment_ids.reshape(per_device, BLOCK), jnp.broadcast_to...]
where the time goes in v3:
time: 73.2 us; the launch traced here: 72.4 us
  Pallas kernels  71.8 us (98%)
    pallas_call x1, Pallas kernels, exchange(): pl.pallas_call(functools.partial(exchange_kernel, n, row_count, head_coun...  67.6 us
    pallas_call x1, Pallas kernels, owned(): pl.pallas_call(functools.partial(owned_kernel, n, per_device), out_shape=...  4.18 us

profile of v3, /device:TPU:3, one launch (start us, length us, event | category | flops | bytes accessed | tf_op | source)
XLA Modules:
  0.0 72.4 jit_solution(9432181843554070661)
XLA Ops:
  0.6 67.6 %shard_map.104 = (bf16[384,2048]{1,0:T(8,128)(2,1)}, bf16[384,4096]{1,0:T(8,128)(2,1)}) custom-call(bf16[256,2048]{1,0:T(8,128)(2,1)} %q_hbm.1, bf16[256,2048]{1,0:T(8,128)(2,1)} %k_hbm.1, bf16[256,2048]{1,0:T(8,128)(2,1)} %v_hbm.1, bf16[256,4096]{1,0:T(8,128)(2,1)} %x_hbm.1, f32[4,4096]{1,0:T(4,128)} %weight_ref.1, f32[1,4096]{1,0:T(1,128)} %bitcast.2, ...), custom_call_target="tpu_custom_call" | custom-call | tf_op jit(solution)/shard_map/pallas_call | solution.py:657
  68.3 4.2 %shard_map.105 = (bf16[384,2048]{1,0:T(8,128)(2,1)}, bf16[384,4096]{1,0:T(8,128)(2,1)}) custom-call(s32[8]{0:T(128)} %counts_ref.1, bf16[384,2048]{1,0:T(8,128)(2,1)} %get-tuple-element.4.attn_near, bf16[384,4096]{1,0:T(8,128)(2,1)} %get-tuple-element.5.conv_near), custom_call_target="tpu_custom_call" | custom-call | tf_op jit(solution)/shard_map/pallas_call | solution.py:758
